TPU v7x, 32 devices: a whole 2x2x4 slice. The times are simulated.
32 devices in a mesh: gx: 2 (over core), gy: 4 (over y, x), gz: 4 (over z).
Axes of the slice: x: 2, y: 2, z: 4, core: 2. Of those that a mesh axis runs over, the one named last changes fastest.
Arguments:
- features: bfloat16 [4096, 512], P(('gx', 'gy', 'gz')), may hold values from -6 to 6
- halo_index: int32 [3072], P(('gx', 'gy', 'gz')), may hold values from 0 to 127
- edge_src: int32 [128, 384], P(('gx', 'gy', 'gz')), may hold values from 0 to 2623
- edge_dst: int32 [128, 384], P(('gx', 'gy', 'gz')), may hold values from 0 to 127
- edge_count: int32 [128], P(('gx', 'gy', 'gz')), may hold values from 48 to 384, as said below
- edge_basis: bfloat16 [49152, 128], P(('gx', 'gy', 'gz')), may hold values from -6 to 6
- w_edge_in: bfloat16 [4, 1152, 1024], P('gz'), may hold values from -0.1875 to 0.1875
- w_edge_out: bfloat16 [4, 1024, 512], P('gz'), may hold values from -0.1875 to 0.1875
- w_update: bfloat16 [512, 512], replicated, may hold values from -0.25 to 0.25
Outputs:
- new_features: bfloat16 [4096, 512], P(('gx', 'gy', 'gz'))
- halo_next: bfloat16 [832, 96, 512], P(('gx', 'gy', 'gz'))
Inputs may be any that keep to these rules, and one draw needn't show every extreme that they name: The first edge_count slots of a domain's 384 slots for a species pair are live; in every draw some species pair has all 384 slots live in every domain of one gz group.
All inputs are finite; a program needn't handle non-finite values.
Results may differ from a plain program's by a relative error of at most 0.0051.
Values may be sent and summed in bfloat16 or wider, within the bound.
A program may use at most 128 MiB of HBM per device.

v0:
```python
import jax
import jax.numpy as jnp
from jax import lax
from jax.sharding import PartitionSpec as P


def extended(x, sides, width):
    for axis, dim in sides:
        count, length = (lax.axis_size(axis), x.shape[dim])
        up = [(i, (i + 1) % count) for i in range(count)]
        down = [(j, i) for i, j in up]
        last = lax.slice_in_dim(x, length - width, length, axis=dim)
        first = lax.slice_in_dim(x, 0, width, axis=dim)
        before = lax.ppermute(last, axis, up)
        after = lax.ppermute(first, axis, down)
        x = jnp.concatenate([before, x, after], axis=dim)
    return x


def outer_cells(padded):
    flat = padded.reshape(27, padded.shape[3], padded.shape[4])
    return jnp.concatenate([flat[:13], flat[14:]], axis=0)


def shards(
    features,
    halo_index,
    edge_src,
    edge_dst,
    edge_count,
    edge_basis,
    w_edge_in,
    w_edge_out,
    w_update,
):
    model_width = features.shape[1]
    atom_count = features.shape[0]
    group_count = edge_src.shape[0]
    slot_count = edge_src.shape[1]
    first_layer = w_edge_in[0]
    w_source = first_layer[:model_width]
    w_target = first_layer[model_width : 2 * model_width]
    w_radial = first_layer[2 * model_width :]
    w_second = w_edge_out[0]
    boundary = features[halo_index]
    padded = extended(boundary[None, None, None], (("gx", 0), ("gy", 1), ("gz", 2)), 1)
    table_rows = jnp.concatenate([features, outer_cells(padded).reshape(-1, model_width)], axis=0)
    slot_index = lax.broadcasted_iota(jnp.int32, (group_count, slot_count), 1)
    dst_live = jnp.where(slot_index < edge_count[:, None], edge_dst, -1)
    src_rows = table_rows[edge_src]
    basis_rows = edge_basis.reshape(group_count, slot_count, -1)
    owners = lax.all_gather(features, "gz", axis=0, tiled=True)
    source_part = lax.all_to_all(src_rows, "gz", split_axis=0, concat_axis=0, tiled=True)
    radial_part = lax.all_to_all(basis_rows, "gz", split_axis=0, concat_axis=0, tiled=True)
    target_part = lax.all_to_all(dst_live, "gz", split_axis=0, concat_axis=0, tiled=True)
    owner_index = lax.broadcasted_iota(jnp.int32, target_part.shape, 0)
    row_index = owner_index * atom_count + jnp.maximum(target_part, 0)
    pre = jnp.einsum("ock,kh->och", source_part, w_source, preferred_element_type=jnp.float32)
    pre = pre + jnp.einsum(
        "ock,kh->och", owners[row_index], w_target, preferred_element_type=jnp.float32
    )
    pre = pre + jnp.einsum("ock,kh->och", radial_part, w_radial, preferred_element_type=jnp.float32)
    hidden = jax.nn.silu(pre).astype(jnp.bfloat16)
    messages = jnp.einsum(
        "och,hd->ocd", hidden, w_second, preferred_element_type=jnp.float32
    ).astype(jnp.bfloat16)
    atom_iota = lax.broadcasted_iota(jnp.int32, (1, atom_count, 1), 1)
    incidence = (target_part[:, None, :] == atom_iota).astype(jnp.bfloat16)
    partial_value = jnp.einsum(
        "oac,ocd->oad", incidence, messages, preferred_element_type=jnp.float32
    )
    returned = lax.all_to_all(partial_value, "gz", split_axis=0, concat_axis=0, tiled=True)
    summed = jnp.sum(returned, axis=0)
    mean_square = jnp.mean(summed * summed, axis=-1, keepdims=True)
    normed = (summed * lax.rsqrt(mean_square + 1e-05)).astype(jnp.bfloat16)
    update = jnp.dot(normed, w_update, preferred_element_type=jnp.float32)
    new_rows = (features.astype(jnp.float32) + update).astype(jnp.bfloat16)
    boundary_next = new_rows[halo_index]
    padded_next = extended(boundary_next[None, None, None], (("gx", 0), ("gy", 1), ("gz", 2)), 1)
    return (new_rows, outer_cells(padded_next))


def solution(mesh):
    in_specs = (
        P(("gx", "gy", "gz"), None),
        P(("gx", "gy", "gz")),
        P(("gx", "gy", "gz"), None),
        P(("gx", "gy", "gz"), None),
        P(("gx", "gy", "gz")),
        P(("gx", "gy", "gz"), None),
        P("gz", None, None),
        P("gz", None, None),
        P(),
    )
    out_specs = (P(("gx", "gy", "gz"), None), P(("gx", "gy", "gz"), None, None))
    return jax.shard_map(shards, mesh=mesh, in_specs=in_specs, out_specs=out_specs, check_vma=False)
```

profile of v0, /device:TPU:0, one launch (start us, length us, event | category | flops | bytes accessed | tf_op | source)
XLA Modules:
  0.0 244.4 jit_solution(17518737411660622284)
XLA Ops:
  1.4 1.7 gather_fusion
  5.0 3.6 %collective-permute-start.3 = (bf16[3,1,1,96,512]{4,3,2,1,0:T(8,128)(2,1)S(1)}, bf16[3,1,1,96,512]{4,3,2,1,0:T(8,128)(2,1)S(1)}, u32[]{:S(2)}, u32[]{:S(2)}) collective-permute-start(bf16[3,1,1,96,512]{4,3,2,1,0:T(8,128)(2,1)S(1)} %pad_maximum_fusion.7), channel_id=1, source_target_pairs={{4,0},{8,4},{12,8},{0,12},{5,1},{9,5},{13,9},{1,13},{6,2},{10,6},{... | collective-permute-start | bytes 884744 | tf_op jit(solution)/shard_map/ppermute | solution.py:15
  8.7 7.4 %collective-permute-done.3 = bf16[3,1,1,96,512]{4,3,2,1,0:T(8,128)(2,1)S(1)} collective-permute-done((bf16[3,1,1,96,512]{4,3,2,1,0:T(8,128)(2,1)S(1)}, bf16[3,1,1,96,512]{4,3,2,1,0:T(8,128)(2,1)S(1)}, u32[]{:S(2)}, u32[]{:S(2)}) %collective-permute-start.3) | collective-permute-done | bytes 294944 | tf_op jit(solution)/shard_map/ppermute | solution.py:15
  16.1 6.7 %collective-permute-done.2 = bf16[3,1,1,96,512]{4,3,2,1,0:T(8,128)(2,1)S(1)} collective-permute-done((bf16[3,1,1,96,512]{4,3,2,1,0:T(8,128)(2,1)S(1)}, bf16[3,1,1,96,512]{4,3,2,1,0:T(8,128)(2,1)S(1)}, u32[]{:S(2)}, u32[]{:S(2)}) %collective-permute-start.2) | collective-permute-done | bytes 294944 | tf_op jit(solution)/shard_map/ppermute | solution.py:14
  22.9 3.7 %collective-permute-start.5 = (bf16[3,3,1,96,512]{4,3,2,1,0:T(8,128)(2,1)S(1)}, bf16[3,3,1,96,512]{4,3,2,1,0:T(8,128)(2,1)S(1)}, u32[]{:S(2)}, u32[]{:S(2)}) collective-permute-start(bf16[3,3,1,96,512]{4,3,2,1,0:T(8,128)(2,1)S(1)} %pad_maximum_fusion.5), channel_id=1, source_target_pairs={{1,0},{2,1},{3,2},{0,3},{5,4},{6,5},{7,6},{4,7},{9,8},{10,9},{11,1... | collective-permute-start | bytes 2654216 | tf_op jit(solution)/shard_map/ppermute | solution.py:15
  27.2 5.1 %all-to-all-start = ((s32[4,1,384]{2,1,0:T(1,128)}), s32[4,1,384]{2,1,0:T(1,128)S(1)}, u32[]{:S(2)}, u32[]{:S(2)}) async-start(s32[4,1,384]{2,1,0:T(1,128)} %all_to_all.15), calls=%async_computation | async-start | bytes 12288 | tf_op jit(solution)/shard_map/all_to_all | solution.py:55
  32.4 14.2 %collective-permute-done.5 = bf16[3,3,1,96,512]{4,3,2,1,0:T(8,128)(2,1)S(1)} collective-permute-done((bf16[3,3,1,96,512]{4,3,2,1,0:T(8,128)(2,1)S(1)}, bf16[3,3,1,96,512]{4,3,2,1,0:T(8,128)(2,1)S(1)}, u32[]{:S(2)}, u32[]{:S(2)}) %collective-permute-start.5) | collective-permute-done | bytes 884768 | tf_op jit(solution)/shard_map/ppermute | solution.py:15
  46.6 18.6 %collective-permute-done.4 = bf16[3,3,1,96,512]{4,3,2,1,0:T(8,128)(2,1)} collective-permute-done((bf16[3,3,1,96,512]{4,3,2,1,0:T(8,128)(2,1)S(1)}, bf16[3,3,1,96,512]{4,3,2,1,0:T(8,128)(2,1)}, u32[]{:S(2)}, u32[]{:S(2)}) %collective-permute-start.4) | collective-permute-done | bytes 884768 | tf_op jit(solution)/shard_map/ppermute | solution.py:14
  67.7 1.7 pad_maximum_fusion
  69.4 7.6 %gather_fusion.1 = bf16[1536,512]{1,0:T(8,128)(2,1)} fusion(bf16[2624,512]{1,0:T(8,128)(2,1)} %pad_maximum_fusion, s32[2048]{0:T(1024)S(1)} %pad_clamp_fusion.1), kind=kCustom, calls=%fused_computation.1 | custom fusion | bytes 3151872 | tf_op jit(solution)/shard_map/gather | solution.py:50
  77.0 3.6 %all-to-all-start.1 = ((bf16[4,384,512]{2,1,0:T(8,128)(2,1)}), bf16[4,384,512]{2,1,0:T(8,128)(2,1)S(1)}, u32[]{:S(2)}, u32[]{:S(2)}) async-start(bf16[4,384,512]{2,1,0:T(8,128)(2,1)} %bitcast.3), calls=%async_computation.1 | async-start | bytes 3145728 | tf_op jit(solution)/shard_map/all_to_all | solution.py:53
  80.5 46.3 %all_gather.3 = bf16[512,512]{1,0:T(8,128)(2,1)S(1)} all-gather(bf16[128,512]{1,0:T(8,128)(2,1)S(1)} %copy-done.1), channel_id=1, replica_groups=mesh['gx'=2,'gy'=4,'gz'=4] {'gz'}, dimensions={0}, use_global_device_ids=true | all-gather | bytes 655360 | tf_op jit(solution)/shard_map/all_gather | solution.py:52
  127.0 5.4 %gather_fusion.2 = bf16[1536,512]{1,0:T(8,128)(2,1)} fusion(bf16[512,512]{1,0:T(8,128)(2,1)S(1)} %all_gather.3, s32[2048]{0:T(1024)S(1)} %pad_clamp_fusion), kind=kCustom, calls=%fused_computation.2 | custom fusion | bytes 3151872 | tf_op jit(solution)/shard_map/gather | solution.py:60
  132.4 4.6 %all-to-all-start.2 = ((bf16[4,384,128]{2,1,0:T(8,128)(2,1)}), bf16[4,384,128]{2,1,0:T(8,128)(2,1)S(1)}, u32[]{:S(2)}, u32[]{:S(2)}) async-start(bf16[4,384,128]{2,1,0:T(8,128)(2,1)} %bitcast.51), calls=%async_computation.2 | async-start | bytes 786432 | tf_op jit(solution)/shard_map/all_to_all | solution.py:54
  137.0 6.2 %fusion.6 = f32[4,384,1024]{2,1,0:T(8,128)} fusion(bf16[4,384,512]{2,1,0:T(8,128)(2,1)} %bitcast.40, bf16[1,1152,1024]{2,1,0:T(8,128)(2,1)} %param.15), kind=kOutput, calls=%fused_computation.16 | convolution fusion | flops 1610612736 | bytes 8912896 | tf_op jit(solution)/shard_map/ock,kh->och/dot_general | solution.py:59
  143.2 5.6 %fusion.8 = f32[4,384,1024]{2,1,0:T(8,128)} fusion(bf16[4,384,512]{2,1,0:T(8,128)(2,1)S(1)} %all-to-all-done.1, bf16[1,1152,1024]{2,1,0:T(8,128)(2,1)} %param.15), kind=kOutput, calls=%fused_computation.18 | convolution fusion | flops 1610612736 | bytes 8912896 | tf_op jit(solution)/shard_map/ock,kh->och/dot_general | solution.py:58
  148.8 8.0 %fusion.3 = bf16[4,384,512]{2,1,0:T(8,128)(2,1)S(1)} fusion(f32[4,384,1024]{2,1,0:T(8,128)} %fusion.8, f32[4,384,1024]{2,1,0:T(8,128)} %fusion.6, bf16[4,384,128]{2,1,0:T(8,128)(2,1)S(1)} %all-to-all-done.2, bf16[1,1024,512]{2,1,0:T(8,128)(2,1)S(1)} %copy-done, bf16[1,1152,1024]{2,1,0:T(8,128)(2,1)} %param.15), kind=kOutput, calls=%fused_computation.12 | convolution fusion | flops 2025062400 | bytes 15859712 | tf_op jit(solution)/shard_map/och,hd->ocd/dot_general | solution.py:64
  157.3 26.3 %all_to_all.24 = f32[4,128,512]{2,1,0:T(8,128)S(1)} all-to-all(f32[4,128,512]{2,1,0:T(8,128)S(1)} %fusion.12), channel_id=1, replica_groups=mesh['gx'=2,'gy'=4,'gz'=4] {'gz'}, dimensions={0} | all-to-all | bytes 2097152 | tf_op jit(solution)/shard_map/all_to_all | solution.py:72
  186.4 1.5 collective-permute-start.9
  188.5 7.9 %collective-permute-done.9 = bf16[3,1,1,96,512]{4,3,2,1,0:T(8,128)(2,1)S(1)} collective-permute-done((bf16[3,1,1,96,512]{4,3,2,1,0:T(8,128)(2,1)S(1)}, bf16[3,1,1,96,512]{4,3,2,1,0:T(8,128)(2,1)S(1)}, u32[]{:S(2)}, u32[]{:S(2)}) %collective-permute-start.9) | collective-permute-done | bytes 294944 | tf_op jit(solution)/shard_map/ppermute | solution.py:15
  196.3 5.7 %collective-permute-done.8 = bf16[3,1,1,96,512]{4,3,2,1,0:T(8,128)(2,1)S(1)} collective-permute-done((bf16[3,1,1,96,512]{4,3,2,1,0:T(8,128)(2,1)S(1)}, bf16[3,1,1,96,512]{4,3,2,1,0:T(8,128)(2,1)S(1)}, u32[]{:S(2)}, u32[]{:S(2)}) %collective-permute-start.8) | collective-permute-done | bytes 294944 | tf_op jit(solution)/shard_map/ppermute | solution.py:14
  202.1 1.5 collective-permute-start.11
  204.2 38.0 %collective-permute-done.11 = bf16[3,3,1,96,512]{4,3,2,1,0:T(8,128)(2,1)S(1)} collective-permute-done((bf16[3,3,1,96,512]{4,3,2,1,0:T(8,128)(2,1)S(1)}, bf16[3,3,1,96,512]{4,3,2,1,0:T(8,128)(2,1)S(1)}, u32[]{:S(2)}, u32[]{:S(2)}) %collective-permute-start.11) | collective-permute-done | bytes 884768 | tf_op jit(solution)/shard_map/ppermute | solution.py:15
  242.7 1.7 pad_maximum_fusion.4
  (61 shorter events, 11.1 us)
Async XLA Ops:
  0.6 148.2 %copy-start = (bf16[1,1024,512]{2,1,0:T(8,128)(2,1)S(1)}, bf16[1,1024,512]{2,1,0:T(8,128)(2,1)}, u32[]{:S(2)}) copy-start(bf16[1,1024,512]{2,1,0:T(8,128)(2,1)} %param.16) | copy-start | bytes 3145732
  0.6 25.9 %copy-start.8 = (s32[4]{0:T(128)S(1)}, s32[4]{0:T(128)}, u32[]{:S(2)}) copy-start(s32[4]{0:T(128)} %param.13) | copy-start | bytes 52
  0.7 25.9 %copy-start.6 = (s32[4,384]{1,0:T(4,128)S(1)}, s32[4,384]{1,0:T(4,128)}, u32[]{:S(2)}) copy-start(s32[4,384]{1,0:T(4,128)} %param.12) | copy-start | bytes 18436
  0.7 31.7 %copy-start.7 = (s32[4,384]{1,0:T(4,128)S(1)}, s32[4,384]{1,0:T(4,128)}, u32[]{:S(2)}) copy-start(s32[4,384]{1,0:T(4,128)} %param.11) | copy-start | bytes 18436
  3.1 1.5 collective-permute-start.1
  3.7 1.3 collective-permute-start
  4.6 21.9 %copy-start.3 = (bf16[1,1,1,96,512]{4,3,2,1,0:T(8,128)(2,1)}, bf16[1,1,1,96,512]{4,3,2,1,0:T(8,128)(2,1)S(1)}, u32[]{:S(2)}) copy-start(bf16[1,1,1,96,512]{4,3,2,1,0:T(8,128)(2,1)S(1)} %collective-permute-done.1) | copy-start | bytes 294916
  5.0 21.6 %copy-start.4 = (bf16[1,1,1,96,512]{4,3,2,1,0:T(8,128)(2,1)}, bf16[1,1,1,96,512]{4,3,2,1,0:T(8,128)(2,1)S(1)}, u32[]{:S(2)}) copy-start(bf16[1,1,1,96,512]{4,3,2,1,0:T(8,128)(2,1)S(1)} %collective-permute-done) | copy-start | bytes 294916
  5.0 11.0 %collective-permute-start.3 = (bf16[3,1,1,96,512]{4,3,2,1,0:T(8,128)(2,1)S(1)}, bf16[3,1,1,96,512]{4,3,2,1,0:T(8,128)(2,1)S(1)}, u32[]{:S(2)}, u32[]{:S(2)}) collective-permute-start(bf16[3,1,1,96,512]{4,3,2,1,0:T(8,128)(2,1)S(1)} %pad_maximum_fusion.7), channel_id=1, source_target_pairs={{4,0},{8,4},{12,8},{0,12},{5,1},{9,5},{13,9},{1,13},{6,2},{10,6},{... | collective-permute-start | bytes 884744 | tf_op jit(solution)/shard_map/ppermute | solution.py:15
  8.7 14.1 %collective-permute-start.2 = (bf16[3,1,1,96,512]{4,3,2,1,0:T(8,128)(2,1)S(1)}, bf16[3,1,1,96,512]{4,3,2,1,0:T(8,128)(2,1)S(1)}, u32[]{:S(2)}, u32[]{:S(2)}) collective-permute-start(bf16[3,1,1,96,512]{4,3,2,1,0:T(8,128)(2,1)S(1)} %pad_maximum_fusion.7), channel_id=1, source_target_pairs={{0,4},{4,8},{8,12},{12,0},{1,5},{5,9},{9,13},{13,1},{2,6},{6,10},{... | collective-permute-start | bytes 884744 | tf_op jit(solution)/shard_map/ppermute | solution.py:14
  22.9 23.7 %collective-permute-start.5 = (bf16[3,3,1,96,512]{4,3,2,1,0:T(8,128)(2,1)S(1)}, bf16[3,3,1,96,512]{4,3,2,1,0:T(8,128)(2,1)S(1)}, u32[]{:S(2)}, u32[]{:S(2)}) collective-permute-start(bf16[3,3,1,96,512]{4,3,2,1,0:T(8,128)(2,1)S(1)} %pad_maximum_fusion.5), channel_id=1, source_target_pairs={{1,0},{2,1},{3,2},{0,3},{5,4},{6,5},{7,6},{4,7},{9,8},{10,9},{11,1... | collective-permute-start | bytes 2654216 | tf_op jit(solution)/shard_map/ppermute | solution.py:15
  26.5 38.6 %collective-permute-start.4 = (bf16[3,3,1,96,512]{4,3,2,1,0:T(8,128)(2,1)S(1)}, bf16[3,3,1,96,512]{4,3,2,1,0:T(8,128)(2,1)}, u32[]{:S(2)}, u32[]{:S(2)}) collective-permute-start(bf16[3,3,1,96,512]{4,3,2,1,0:T(8,128)(2,1)S(1)} %pad_maximum_fusion.5), channel_id=1, source_target_pairs={{0,1},{1,2},{2,3},{3,0},{4,5},{5,6},{6,7},{7,4},{8,9},{9,10},{10,1... | collective-permute-start | bytes 2654216 | tf_op jit(solution)/shard_map/ppermute | solution.py:14
  27.2 49.7 %all-to-all-start = ((s32[4,1,384]{2,1,0:T(1,128)}), s32[4,1,384]{2,1,0:T(1,128)S(1)}, u32[]{:S(2)}, u32[]{:S(2)}) async-start(s32[4,1,384]{2,1,0:T(1,128)} %all_to_all.15), calls=%async_computation | async-start | bytes 12288 | tf_op jit(solution)/shard_map/all_to_all | solution.py:55
  66.7 0.9 copy-start.1
  77.0 55.5 %all-to-all-start.1 = ((bf16[4,384,512]{2,1,0:T(8,128)(2,1)}), bf16[4,384,512]{2,1,0:T(8,128)(2,1)S(1)}, u32[]{:S(2)}, u32[]{:S(2)}) async-start(bf16[4,384,512]{2,1,0:T(8,128)(2,1)} %bitcast.3), calls=%async_computation.1 | async-start | bytes 3145728 | tf_op jit(solution)/shard_map/all_to_all | solution.py:53
  132.4 16.4 %all-to-all-start.2 = ((bf16[4,384,128]{2,1,0:T(8,128)(2,1)}), bf16[4,384,128]{2,1,0:T(8,128)(2,1)S(1)}, u32[]{:S(2)}, u32[]{:S(2)}) async-start(bf16[4,384,128]{2,1,0:T(8,128)(2,1)} %bitcast.51), calls=%async_computation.2 | async-start | bytes 786432 | tf_op jit(solution)/shard_map/all_to_all | solution.py:54
  156.8 26.9 %copy-start.5 = (bf16[512,512]{1,0:T(8,128)(2,1)S(1)}, bf16[512,512]{1,0:T(8,128)(2,1)}, u32[]{:S(2)}) copy-start(bf16[512,512]{1,0:T(8,128)(2,1)} %param.17) | copy-start | bytes 1572868
  184.0 58.5 %copy-start.2 = (bf16[128,512]{1,0:T(8,128)(2,1)}, bf16[128,512]{1,0:T(8,128)(2,1)S(1)}, u32[]{:S(2)}) copy-start(bf16[128,512]{1,0:T(8,128)(2,1)S(1)} %fusion.4) | copy-start | bytes 393220
  184.8 1.4 collective-permute-start.7
  184.9 1.4 collective-permute-start.6
  186.4 9.9 %collective-permute-start.9 = (bf16[3,1,1,96,512]{4,3,2,1,0:T(8,128)(2,1)S(1)}, bf16[3,1,1,96,512]{4,3,2,1,0:T(8,128)(2,1)S(1)}, u32[]{:S(2)}, u32[]{:S(2)}) collective-permute-start(bf16[3,1,1,96,512]{4,3,2,1,0:T(8,128)(2,1)S(1)} %pad_maximum_fusion.8), channel_id=1, source_target_pairs={{4,0},{8,4},{12,8},{0,12},{5,1},{9,5},{13,9},{1,13},{6,2},{10,6},{... | collective-permute-start | bytes 884744 | tf_op jit(solution)/shard_map/ppermute | solution.py:15
  187.9 14.1 %collective-permute-start.8 = (bf16[3,1,1,96,512]{4,3,2,1,0:T(8,128)(2,1)S(1)}, bf16[3,1,1,96,512]{4,3,2,1,0:T(8,128)(2,1)S(1)}, u32[]{:S(2)}, u32[]{:S(2)}) collective-permute-start(bf16[3,1,1,96,512]{4,3,2,1,0:T(8,128)(2,1)S(1)} %pad_maximum_fusion.8), channel_id=1, source_target_pairs={{0,4},{4,8},{8,12},{12,0},{1,5},{5,9},{9,13},{13,1},{2,6},{6,10},{... | collective-permute-start | bytes 884744 | tf_op jit(solution)/shard_map/ppermute | solution.py:14
  202.1 40.1 %collective-permute-start.11 = (bf16[3,3,1,96,512]{4,3,2,1,0:T(8,128)(2,1)S(1)}, bf16[3,3,1,96,512]{4,3,2,1,0:T(8,128)(2,1)S(1)}, u32[]{:S(2)}, u32[]{:S(2)}) collective-permute-start(bf16[3,3,1,96,512]{4,3,2,1,0:T(8,128)(2,1)S(1)} %pad_maximum_fusion.6), channel_id=1, source_target_pairs={{1,0},{2,1},{3,2},{0,3},{5,4},{6,5},{7,6},{4,7},{9,8},{10,9},{11,1... | collective-permute-start | bytes 2654216 | tf_op jit(solution)/shard_map/ppermute | solution.py:15
  203.6 38.6 %collective-permute-start.10 = (bf16[3,3,1,96,512]{4,3,2,1,0:T(8,128)(2,1)S(1)}, bf16[3,3,1,96,512]{4,3,2,1,0:T(8,128)(2,1)S(1)}, u32[]{:S(2)}, u32[]{:S(2)}) collective-permute-start(bf16[3,3,1,96,512]{4,3,2,1,0:T(8,128)(2,1)S(1)} %pad_maximum_fusion.6), channel_id=1, source_target_pairs={{0,1},{1,2},{2,3},{3,0},{4,5},{5,6},{6,7},{7,4},{8,9},{9,10},{10,1... | collective-permute-start | bytes 2654216 | tf_op jit(solution)/shard_map/ppermute | solution.py:14
where the time goes:
time: 245 us; the launch traced here: 244 us
  waiting for transfers between devices  101 us (41%)
  blocking collectives  72.6 us (30%)
  starting transfers between devices  25.9 us (11%)
  matrix products  20.5 us (8%)
  local copies, waits for them, and re-layouts  17.2 us (7%)
  other arithmetic  6.8 us (3%)
    ppermute x6, waiting for transfers between devices, extended(): after = lax.ppermute(first, axis, down)  69.1 us
    all_gather x1, blocking collectives, shards(): owners = lax.all_gather(features, 'gz', axis=0, tiled=True)  46.3 us
    ppermute x6, waiting for transfers between devices, extended(): before = lax.ppermute(last, axis, up)  31.4 us
    all_to_all x1, blocking collectives, shards(): lax.all_to_all(partial_value, 'gz', split_axis=0, concat_axis=0, tiled=True)  26.3 us
    ppermute x6, starting transfers between devices, extended(): after = lax.ppermute(first, axis, down)  10.9 us
    dot_general x1, matrix products, shards(): jnp.einsum('och,hd->ocd', hidden, w_second, preferred_element_type=jnp.fl...  7.98 us
    gather x1, local copies, waits for them, and re-layouts, shards(): src_rows = table_rows[edge_src]  7.59 us
    dot_general x1, matrix products, shards(): jnp.einsum('ock,kh->och', owners[row_index], w_target, preferred_element_...  6.17 us
  transfers between devices with their start and end apart: 15, of which 11 were waited for; matrix products, arithmetic and copies ran while one was open for 12% of the time, Pallas kernels for 0%

commit v1 on v0

--- a/solution.py
+++ b/solution.py
@@ -49,7 +49,12 @@
     dst_live = jnp.where(slot_index < edge_count[:, None], edge_dst, -1)
     src_rows = table_rows[edge_src]
     basis_rows = edge_basis.reshape(group_count, slot_count, -1)
-    owners = lax.all_gather(features, "gz", axis=0, tiled=True)
+    ring = [features]
+    for hop in range(3):
+        ring.append(lax.ppermute(ring[-1], "gz", [(dev, (dev + 1) % 4) for dev in range(4)]))
+    owners = jnp.roll(
+        jnp.concatenate(ring[::-1], axis=0), (lax.axis_index("gz") + 1) * ring[0].shape[0], axis=0
+    )
     source_part = lax.all_to_all(src_rows, "gz", split_axis=0, concat_axis=0, tiled=True)
     radial_part = lax.all_to_all(basis_rows, "gz", split_axis=0, concat_axis=0, tiled=True)
     target_part = lax.all_to_all(dst_live, "gz", split_axis=0, concat_axis=0, tiled=True)

time: 245 us -> 246 us (level)
  blocking collectives: 72.6 us -> 25.2 us
  waiting for transfers between devices: 101 us -> 138 us
  starting transfers between devices: 25.9 us -> 37.1 us
    all_gather x1 -> x0, blocking collectives: 46.3 us -> none  [shards(): owners = lax.all_gather(features, 'gz', axis=0, tiled=True)]
    ppermute x0 -> x3, waiting for transfers between devices: none -> 37 us  [shards(): lax.ppermute(ring[-1], 'gz', [(dev, (dev + 1) % 4) for dev in range(4)])]
    all_to_all x1, waiting for transfers between devices: 0.01 us -> 32.8 us  [shards(): lax.all_to_all(dst_live, 'gz', split_axis=0, concat_axis=0, tiled=True)]
    ppermute x6, waiting for transfers between devices: 31.4 us -> 12.9 us  [extended(): before = lax.ppermute(last, axis, up)]
    ppermute x6, waiting for transfers between devices: 69.1 us -> 54.9 us  [extended(): after = lax.ppermute(first, axis, down)]
    ppermute x0 -> x3, starting transfers between devices: none -> 11 us  [shards(): lax.ppermute(ring[-1], 'gz', [(dev, (dev + 1) % 4) for dev in range(4)])]
  transfers between devices with their start and end apart: 15 -> 18, of which waited for: 11 -> 13; matrix products, arithmetic and copies ran while one was open for 12% -> 7% of each run, Pallas kernels for 0% -> 0%
where the time goes in v1:
time: 246 us; the launch traced here: 245 us
  waiting for transfers between devices  138 us (56%)
  starting transfers between devices  37.1 us (15%)
  blocking collectives  25.2 us (10%)
  matrix products  20.5 us (8%)
  local copies, waits for them, and re-layouts  17.3 us (7%)
  other arithmetic  6.8 us (3%)
    ppermute x6, waiting for transfers between devices, extended(): after = lax.ppermute(first, axis, down)  54.9 us
    ppermute x3, waiting for transfers between devices, shards(): lax.ppermute(ring[-1], 'gz', [(dev, (dev + 1) % 4) for dev in range(4)])  37 us
    all_to_all x1, waiting for transfers between devices, shards(): lax.all_to_all(dst_live, 'gz', split_axis=0, concat_axis=0, tiled=True)  32.8 us
    all_to_all x1, blocking collectives, shards(): lax.all_to_all(partial_value, 'gz', split_axis=0, concat_axis=0, tiled=True)  25.2 us
    ppermute x6, waiting for transfers between devices, extended(): before = lax.ppermute(last, axis, up)  12.9 us
    ppermute x3, starting transfers between devices, shards(): lax.ppermute(ring[-1], 'gz', [(dev, (dev + 1) % 4) for dev in range(4)])  11 us
    ppermute x6, starting transfers between devices, extended(): after = lax.ppermute(first, axis, down)  10.9 us
    dot_general x1, matrix products, shards(): jnp.einsum('och,hd->ocd', hidden, w_second, preferred_element_type=jnp.fl...  7.98 us
  transfers between devices with their start and end apart: 18, of which 13 were waited for; matrix products, arithmetic and copies ran while one was open for 7% of the time, Pallas kernels for 0%

profile of v1, /device:TPU:0, one launch (start us, length us, event | category | flops | bytes accessed | tf_op | source)
XLA Modules:
  0.0 245.3 jit_solution(9217928876491454360)
XLA Ops:
  1.4 1.7 gather_fusion
  5.0 3.6 %collective-permute-start.3 = (bf16[3,1,1,96,512]{4,3,2,1,0:T(8,128)(2,1)S(1)}, bf16[3,1,1,96,512]{4,3,2,1,0:T(8,128)(2,1)S(1)}, u32[]{:S(2)}, u32[]{:S(2)}) collective-permute-start(bf16[3,1,1,96,512]{4,3,2,1,0:T(8,128)(2,1)S(1)} %pad_maximum_fusion.7), channel_id=1, source_target_pairs={{4,0},{8,4},{12,8},{0,12},{5,1},{9,5},{13,9},{1,13},{6,2},{10,6},{... | collective-permute-start | bytes 884744 | tf_op jit(solution)/shard_map/ppermute | solution.py:15
  8.7 7.4 %collective-permute-done.3 = bf16[3,1,1,96,512]{4,3,2,1,0:T(8,128)(2,1)S(1)} collective-permute-done((bf16[3,1,1,96,512]{4,3,2,1,0:T(8,128)(2,1)S(1)}, bf16[3,1,1,96,512]{4,3,2,1,0:T(8,128)(2,1)S(1)}, u32[]{:S(2)}, u32[]{:S(2)}) %collective-permute-start.3) | collective-permute-done | bytes 294944 | tf_op jit(solution)/shard_map/ppermute | solution.py:15
  16.1 6.7 %collective-permute-done.2 = bf16[3,1,1,96,512]{4,3,2,1,0:T(8,128)(2,1)S(1)} collective-permute-done((bf16[3,1,1,96,512]{4,3,2,1,0:T(8,128)(2,1)S(1)}, bf16[3,1,1,96,512]{4,3,2,1,0:T(8,128)(2,1)S(1)}, u32[]{:S(2)}, u32[]{:S(2)}) %collective-permute-start.2) | collective-permute-done | bytes 294944 | tf_op jit(solution)/shard_map/ppermute | solution.py:14
  22.9 3.7 %collective-permute-start.5 = (bf16[3,3,1,96,512]{4,3,2,1,0:T(8,128)(2,1)S(1)}, bf16[3,3,1,96,512]{4,3,2,1,0:T(8,128)(2,1)S(1)}, u32[]{:S(2)}, u32[]{:S(2)}) collective-permute-start(bf16[3,3,1,96,512]{4,3,2,1,0:T(8,128)(2,1)S(1)} %pad_maximum_fusion.5), channel_id=1, source_target_pairs={{1,0},{2,1},{3,2},{0,3},{5,4},{6,5},{7,6},{4,7},{9,8},{10,9},{11,1... | collective-permute-start | bytes 2654216 | tf_op jit(solution)/shard_map/ppermute | solution.py:15
  27.2 5.1 %all-to-all-start = ((s32[4,1,384]{2,1,0:T(1,128)}), s32[4,1,384]{2,1,0:T(1,128)S(1)}, u32[]{:S(2)}, u32[]{:S(2)}) async-start(s32[4,1,384]{2,1,0:T(1,128)} %all_to_all.15), calls=%async_computation | async-start | bytes 12288 | tf_op jit(solution)/shard_map/all_to_all | solution.py:60
  32.4 32.8 %all-to-all-done = s32[4,1,384]{2,1,0:T(1,128)S(1)} async-done(((s32[4,1,384]{2,1,0:T(1,128)}), s32[4,1,384]{2,1,0:T(1,128)S(1)}, u32[]{:S(2)}, u32[]{:S(2)}) %all-to-all-start) | async-done | bytes 6176 | tf_op jit(solution)/shard_map/all_to_all | solution.py:60
  69.5 7.6 %gather_fusion.1 = bf16[1536,512]{1,0:T(8,128)(2,1)} fusion(bf16[2624,512]{1,0:T(8,128)(2,1)} %pad_maximum_fusion, s32[2048]{0:T(1024)S(1)} %get-tuple-element.7), kind=kCustom, calls=%fused_computation.1 | custom fusion | bytes 3151872 | tf_op jit(solution)/shard_map/gather | solution.py:50
  77.1 4.6 %all-to-all-start.1 = ((bf16[4,384,512]{2,1,0:T(8,128)(2,1)}), bf16[4,384,512]{2,1,0:T(8,128)(2,1)S(1)}, u32[]{:S(2)}, u32[]{:S(2)}) async-start(bf16[4,384,512]{2,1,0:T(8,128)(2,1)} %bitcast.3), calls=%async_computation.1 | async-start | bytes 3145728 | tf_op jit(solution)/shard_map/all_to_all | solution.py:58
  81.7 2.0 collective-permute-start.6
  83.7 28.9 %collective-permute-done.6 = bf16[128,512]{1,0:T(8,128)(2,1)S(1)} collective-permute-done((bf16[128,512]{1,0:T(8,128)(2,1)S(1)}, bf16[128,512]{1,0:T(8,128)(2,1)S(1)}, u32[]{:S(2)}, u32[]{:S(2)}) %collective-permute-start.6) | collective-permute-done | bytes 131104 | tf_op jit(solution)/shard_map/ppermute | solution.py:54
  112.6 6.5 %collective-permute-start.7 = (bf16[128,512]{1,0:T(8,128)(2,1)S(1)}, bf16[128,512]{1,0:T(8,128)(2,1)S(1)}, u32[]{:S(2)}, u32[]{:S(2)}) collective-permute-start(bf16[128,512]{1,0:T(8,128)(2,1)S(1)} %collective-permute-done.6), channel_id=1, source_target_pairs={{0,1},{1,2},{2,3},{3,0},{4,5},{5,6},{6,7},{7,4},{8,9},{9,10},{10,1... | collective-permute-start | bytes 393224 | tf_op jit(solution)/shard_map/ppermute | solution.py:54
  119.1 3.8 %collective-permute-done.7 = bf16[128,512]{1,0:T(8,128)(2,1)S(1)} collective-permute-done((bf16[128,512]{1,0:T(8,128)(2,1)S(1)}, bf16[128,512]{1,0:T(8,128)(2,1)S(1)}, u32[]{:S(2)}, u32[]{:S(2)}) %collective-permute-start.7) | collective-permute-done | bytes 131104 | tf_op jit(solution)/shard_map/ppermute | solution.py:54
  122.9 2.5 %collective-permute-start.8 = (bf16[128,512]{1,0:T(8,128)(2,1)S(1)}, bf16[128,512]{1,0:T(8,128)(2,1)S(1)}, u32[]{:S(2)}, u32[]{:S(2)}) collective-permute-start(bf16[128,512]{1,0:T(8,128)(2,1)S(1)} %collective-permute-done.7), channel_id=1, source_target_pairs={{0,1},{1,2},{2,3},{3,0},{4,5},{5,6},{6,7},{7,4},{8,9},{9,10},{10,1... | collective-permute-start | bytes 393224 | tf_op jit(solution)/shard_map/ppermute | solution.py:54
  125.4 4.3 %collective-permute-done.8 = bf16[128,512]{1,0:T(8,128)(2,1)S(1)} collective-permute-done((bf16[128,512]{1,0:T(8,128)(2,1)S(1)}, bf16[128,512]{1,0:T(8,128)(2,1)S(1)}, u32[]{:S(2)}, u32[]{:S(2)}) %collective-permute-start.8) | collective-permute-done | bytes 131104 | tf_op jit(solution)/shard_map/ppermute | solution.py:54
  129.9 5.4 %gather_fusion.2 = bf16[1536,512]{1,0:T(8,128)(2,1)} fusion(bf16[512,512]{1,0:T(8,128)(2,1)S(1)} %constant_dynamic-slice_fusion, s32[2048]{0:T(1024)S(1)} %get-tuple-element.6), kind=kCustom, calls=%fused_computation.2 | custom fusion | bytes 3151872 | tf_op jit(solution)/shard_map/gather | solution.py:65
  135.3 3.7 %all-to-all-start.2 = ((bf16[4,384,128]{2,1,0:T(8,128)(2,1)}), bf16[4,384,128]{2,1,0:T(8,128)(2,1)S(1)}, u32[]{:S(2)}, u32[]{:S(2)}) async-start(bf16[4,384,128]{2,1,0:T(8,128)(2,1)} %bitcast.51), calls=%async_computation.2 | async-start | bytes 786432 | tf_op jit(solution)/shard_map/all_to_all | solution.py:59
  139.1 6.2 %fusion.6 = f32[4,384,1024]{2,1,0:T(8,128)} fusion(bf16[4,384,512]{2,1,0:T(8,128)(2,1)} %bitcast.40, bf16[1,1152,1024]{2,1,0:T(8,128)(2,1)} %param.15), kind=kOutput, calls=%fused_computation.16 | convolution fusion | flops 1610612736 | bytes 8912896 | tf_op jit(solution)/shard_map/ock,kh->och/dot_general | solution.py:64
  145.2 5.6 %fusion.8 = f32[4,384,1024]{2,1,0:T(8,128)} fusion(bf16[4,384,512]{2,1,0:T(8,128)(2,1)S(1)} %all-to-all-done.1, bf16[1,1152,1024]{2,1,0:T(8,128)(2,1)} %param.15), kind=kOutput, calls=%fused_computation.18 | convolution fusion | flops 1610612736 | bytes 8912896 | tf_op jit(solution)/shard_map/ock,kh->och/dot_general | solution.py:63
  150.9 8.0 %fusion.3 = bf16[4,384,512]{2,1,0:T(8,128)(2,1)S(1)} fusion(f32[4,384,1024]{2,1,0:T(8,128)} %fusion.8, f32[4,384,1024]{2,1,0:T(8,128)} %fusion.6, bf16[4,384,128]{2,1,0:T(8,128)(2,1)S(1)} %all-to-all-done.2, bf16[1,1024,512]{2,1,0:T(8,128)(2,1)S(1)} %copy-done, bf16[1,1152,1024]{2,1,0:T(8,128)(2,1)} %param.15), kind=kOutput, calls=%fused_computation.12 | convolution fusion | flops 2025062400 | bytes 15859712 | tf_op jit(solution)/shard_map/och,hd->ocd/dot_general | solution.py:69
  159.3 25.2 %all_to_all.24 = f32[4,128,512]{2,1,0:T(8,128)S(1)} all-to-all(f32[4,128,512]{2,1,0:T(8,128)S(1)} %fusion.12), channel_id=1, replica_groups=mesh['gx'=2,'gy'=4,'gz'=4] {'gz'}, dimensions={0} | all-to-all | bytes 2097152 | tf_op jit(solution)/shard_map/all_to_all | solution.py:77
  189.4 7.9 %collective-permute-done.12 = bf16[3,1,1,96,512]{4,3,2,1,0:T(8,128)(2,1)S(1)} collective-permute-done((bf16[3,1,1,96,512]{4,3,2,1,0:T(8,128)(2,1)S(1)}, bf16[3,1,1,96,512]{4,3,2,1,0:T(8,128)(2,1)S(1)}, u32[]{:S(2)}, u32[]{:S(2)}) %collective-permute-start.12) | collective-permute-done | bytes 294944 | tf_op jit(solution)/shard_map/ppermute | solution.py:15
  197.3 5.7 %collective-permute-done.11 = bf16[3,1,1,96,512]{4,3,2,1,0:T(8,128)(2,1)S(1)} collective-permute-done((bf16[3,1,1,96,512]{4,3,2,1,0:T(8,128)(2,1)S(1)}, bf16[3,1,1,96,512]{4,3,2,1,0:T(8,128)(2,1)S(1)}, u32[]{:S(2)}, u32[]{:S(2)}) %collective-permute-start.11) | collective-permute-done | bytes 294944 | tf_op jit(solution)/shard_map/ppermute | solution.py:14
  205.1 38.0 %collective-permute-done.14 = bf16[3,3,1,96,512]{4,3,2,1,0:T(8,128)(2,1)S(1)} collective-permute-done((bf16[3,3,1,96,512]{4,3,2,1,0:T(8,128)(2,1)S(1)}, bf16[3,3,1,96,512]{4,3,2,1,0:T(8,128)(2,1)S(1)}, u32[]{:S(2)}, u32[]{:S(2)}) %collective-permute-start.14) | collective-permute-done | bytes 884768 | tf_op jit(solution)/shard_map/ppermute | solution.py:15
  (74 shorter events, 17.6 us)
Async XLA Ops:
  0.6 150.3 %copy-start = (bf16[1,1024,512]{2,1,0:T(8,128)(2,1)S(1)}, bf16[1,1024,512]{2,1,0:T(8,128)(2,1)}, u32[]{:S(2)}) copy-start(bf16[1,1024,512]{2,1,0:T(8,128)(2,1)} %param.16) | copy-start | bytes 3145732
  0.6 25.9 %copy-start.8 = (s32[4]{0:T(128)S(1)}, s32[4]{0:T(128)}, u32[]{:S(2)}) copy-start(s32[4]{0:T(128)} %param.13) | copy-start | bytes 52
  0.7 25.9 %copy-start.6 = (s32[4,384]{1,0:T(4,128)S(1)}, s32[4,384]{1,0:T(4,128)}, u32[]{:S(2)}) copy-start(s32[4,384]{1,0:T(4,128)} %param.12) | copy-start | bytes 18436
  0.7 31.7 %copy-start.7 = (s32[4,384]{1,0:T(4,128)S(1)}, s32[4,384]{1,0:T(4,128)}, u32[]{:S(2)}) copy-start(s32[4,384]{1,0:T(4,128)} %param.11) | copy-start | bytes 18436
  3.1 1.5 collective-permute-start.1
  3.7 1.3 collective-permute-start
  5.0 11.0 %collective-permute-start.3 = (bf16[3,1,1,96,512]{4,3,2,1,0:T(8,128)(2,1)S(1)}, bf16[3,1,1,96,512]{4,3,2,1,0:T(8,128)(2,1)S(1)}, u32[]{:S(2)}, u32[]{:S(2)}) collective-permute-start(bf16[3,1,1,96,512]{4,3,2,1,0:T(8,128)(2,1)S(1)} %pad_maximum_fusion.7), channel_id=1, source_target_pairs={{4,0},{8,4},{12,8},{0,12},{5,1},{9,5},{13,9},{1,13},{6,2},{10,6},{... | collective-permute-start | bytes 884744 | tf_op jit(solution)/shard_map/ppermute | solution.py:15
  8.7 14.1 %collective-permute-start.2 = (bf16[3,1,1,96,512]{4,3,2,1,0:T(8,128)(2,1)S(1)}, bf16[3,1,1,96,512]{4,3,2,1,0:T(8,128)(2,1)S(1)}, u32[]{:S(2)}, u32[]{:S(2)}) collective-permute-start(bf16[3,1,1,96,512]{4,3,2,1,0:T(8,128)(2,1)S(1)} %pad_maximum_fusion.7), channel_id=1, source_target_pairs={{0,4},{4,8},{8,12},{12,0},{1,5},{5,9},{9,13},{13,1},{2,6},{6,10},{... | collective-permute-start | bytes 884744 | tf_op jit(solution)/shard_map/ppermute | solution.py:14
  22.9 42.4 %collective-permute-start.5 = (bf16[3,3,1,96,512]{4,3,2,1,0:T(8,128)(2,1)S(1)}, bf16[3,3,1,96,512]{4,3,2,1,0:T(8,128)(2,1)S(1)}, u32[]{:S(2)}, u32[]{:S(2)}) collective-permute-start(bf16[3,3,1,96,512]{4,3,2,1,0:T(8,128)(2,1)S(1)} %pad_maximum_fusion.5), channel_id=1, source_target_pairs={{1,0},{2,1},{3,2},{0,3},{5,4},{6,5},{7,6},{4,7},{9,8},{10,9},{11,1... | collective-permute-start | bytes 2654216 | tf_op jit(solution)/shard_map/ppermute | solution.py:15
  26.5 38.7 %collective-permute-start.4 = (bf16[3,3,1,96,512]{4,3,2,1,0:T(8,128)(2,1)S(1)}, bf16[3,3,1,96,512]{4,3,2,1,0:T(8,128)(2,1)}, u32[]{:S(2)}, u32[]{:S(2)}) collective-permute-start(bf16[3,3,1,96,512]{4,3,2,1,0:T(8,128)(2,1)S(1)} %pad_maximum_fusion.5), channel_id=1, source_target_pairs={{0,1},{1,2},{2,3},{3,0},{4,5},{5,6},{6,7},{7,4},{8,9},{9,10},{10,1... | collective-permute-start | bytes 2654216 | tf_op jit(solution)/shard_map/ppermute | solution.py:14
  27.2 37.9 %all-to-all-start = ((s32[4,1,384]{2,1,0:T(1,128)}), s32[4,1,384]{2,1,0:T(1,128)S(1)}, u32[]{:S(2)}, u32[]{:S(2)}) async-start(s32[4,1,384]{2,1,0:T(1,128)} %all_to_all.15), calls=%async_computation | async-start | bytes 12288 | tf_op jit(solution)/shard_map/all_to_all | solution.py:60
  77.1 58.2 %all-to-all-start.1 = ((bf16[4,384,512]{2,1,0:T(8,128)(2,1)}), bf16[4,384,512]{2,1,0:T(8,128)(2,1)S(1)}, u32[]{:S(2)}, u32[]{:S(2)}) async-start(bf16[4,384,512]{2,1,0:T(8,128)(2,1)} %bitcast.3), calls=%async_computation.1 | async-start | bytes 3145728 | tf_op jit(solution)/shard_map/all_to_all | solution.py:58
  81.7 30.9 %collective-permute-start.6 = (bf16[128,512]{1,0:T(8,128)(2,1)S(1)}, bf16[128,512]{1,0:T(8,128)(2,1)S(1)}, u32[]{:S(2)}, u32[]{:S(2)}) collective-permute-start(bf16[128,512]{1,0:T(8,128)(2,1)S(1)} %copy-done.1), channel_id=1, source_target_pairs={{0,1},{1,2},{2,3},{3,0},{4,5},{5,6},{6,7},{7,4},{8,9},{9,10},{10,1... | collective-permute-start | bytes 393224 | tf_op jit(solution)/shard_map/ppermute | solution.py:54
  112.6 10.3 %collective-permute-start.7 = (bf16[128,512]{1,0:T(8,128)(2,1)S(1)}, bf16[128,512]{1,0:T(8,128)(2,1)S(1)}, u32[]{:S(2)}, u32[]{:S(2)}) collective-permute-start(bf16[128,512]{1,0:T(8,128)(2,1)S(1)} %collective-permute-done.6), channel_id=1, source_target_pairs={{0,1},{1,2},{2,3},{3,0},{4,5},{5,6},{6,7},{7,4},{8,9},{9,10},{10,1... | collective-permute-start | bytes 393224 | tf_op jit(solution)/shard_map/ppermute | solution.py:54
  122.9 6.8 %collective-permute-start.8 = (bf16[128,512]{1,0:T(8,128)(2,1)S(1)}, bf16[128,512]{1,0:T(8,128)(2,1)S(1)}, u32[]{:S(2)}, u32[]{:S(2)}) collective-permute-start(bf16[128,512]{1,0:T(8,128)(2,1)S(1)} %collective-permute-done.7), channel_id=1, source_target_pairs={{0,1},{1,2},{2,3},{3,0},{4,5},{5,6},{6,7},{7,4},{8,9},{9,10},{10,1... | collective-permute-start | bytes 393224 | tf_op jit(solution)/shard_map/ppermute | solution.py:54
  135.3 15.5 %all-to-all-start.2 = ((bf16[4,384,128]{2,1,0:T(8,128)(2,1)}), bf16[4,384,128]{2,1,0:T(8,128)(2,1)S(1)}, u32[]{:S(2)}, u32[]{:S(2)}) async-start(bf16[4,384,128]{2,1,0:T(8,128)(2,1)} %bitcast.51), calls=%async_computation.2 | async-start | bytes 786432 | tf_op jit(solution)/shard_map/all_to_all | solution.py:59
  158.9 25.8 %copy-start.5 = (bf16[512,512]{1,0:T(8,128)(2,1)S(1)}, bf16[512,512]{1,0:T(8,128)(2,1)}, u32[]{:S(2)}) copy-start(bf16[512,512]{1,0:T(8,128)(2,1)} %param.17) | copy-start | bytes 1572868
  185.0 58.5 %copy-start.2 = (bf16[128,512]{1,0:T(8,128)(2,1)}, bf16[128,512]{1,0:T(8,128)(2,1)S(1)}, u32[]{:S(2)}) copy-start(bf16[128,512]{1,0:T(8,128)(2,1)S(1)} %fusion.4) | copy-start | bytes 393220
  185.8 1.4 collective-permute-start.10
  185.9 1.4 collective-permute-start.9
  187.3 9.9 %collective-permute-start.12 = (bf16[3,1,1,96,512]{4,3,2,1,0:T(8,128)(2,1)S(1)}, bf16[3,1,1,96,512]{4,3,2,1,0:T(8,128)(2,1)S(1)}, u32[]{:S(2)}, u32[]{:S(2)}) collective-permute-start(bf16[3,1,1,96,512]{4,3,2,1,0:T(8,128)(2,1)S(1)} %pad_maximum_fusion.8), channel_id=1, source_target_pairs={{4,0},{8,4},{12,8},{0,12},{5,1},{9,5},{13,9},{1,13},{6,2},{10,6},{... | collective-permute-start | bytes 884744 | tf_op jit(solution)/shard_map/ppermute | solution.py:15
  188.8 14.1 %collective-permute-start.11 = (bf16[3,1,1,96,512]{4,3,2,1,0:T(8,128)(2,1)S(1)}, bf16[3,1,1,96,512]{4,3,2,1,0:T(8,128)(2,1)S(1)}, u32[]{:S(2)}, u32[]{:S(2)}) collective-permute-start(bf16[3,1,1,96,512]{4,3,2,1,0:T(8,128)(2,1)S(1)} %pad_maximum_fusion.8), channel_id=1, source_target_pairs={{0,4},{4,8},{8,12},{12,0},{1,5},{5,9},{9,13},{13,1},{2,6},{6,10},{... | collective-permute-start | bytes 884744 | tf_op jit(solution)/shard_map/ppermute | solution.py:14
  203.0 40.1 %collective-permute-start.14 = (bf16[3,3,1,96,512]{4,3,2,1,0:T(8,128)(2,1)S(1)}, bf16[3,3,1,96,512]{4,3,2,1,0:T(8,128)(2,1)S(1)}, u32[]{:S(2)}, u32[]{:S(2)}) collective-permute-start(bf16[3,3,1,96,512]{4,3,2,1,0:T(8,128)(2,1)S(1)} %pad_maximum_fusion.6), channel_id=1, source_target_pairs={{1,0},{2,1},{3,2},{0,3},{5,4},{6,5},{7,6},{4,7},{9,8},{10,9},{11,1... | collective-permute-start | bytes 2654216 | tf_op jit(solution)/shard_map/ppermute | solution.py:15
  204.6 38.6 %collective-permute-start.13 = (bf16[3,3,1,96,512]{4,3,2,1,0:T(8,128)(2,1)S(1)}, bf16[3,3,1,96,512]{4,3,2,1,0:T(8,128)(2,1)S(1)}, u32[]{:S(2)}, u32[]{:S(2)}) collective-permute-start(bf16[3,3,1,96,512]{4,3,2,1,0:T(8,128)(2,1)S(1)} %pad_maximum_fusion.6), channel_id=1, source_target_pairs={{0,1},{1,2},{2,3},{3,0},{4,5},{5,6},{6,7},{7,4},{8,9},{9,10},{10,1... | collective-permute-start | bytes 2654216 | tf_op jit(solution)/shard_map/ppermute | solution.py:14
  (3 other events, 44.4 us)
